TPU v7x, 32 devices: a whole 2x2x4 slice. The times are simulated.
32 devices in a mesh: groups: 2 (over y), ctx: 4 (over z), kvh: 2 (over x), rep: 2 (over core).
Axes of the slice: x: 2, y: 2, z: 4, core: 2. Of those that a mesh axis runs over, the one named last changes fastest.
Arguments:
- context_queries: bfloat16 [8192, 8192], P(('groups', 'ctx'), ('kvh', 'rep')), parts along dimension 0, may hold values from -128 to 128
- context_keys: bfloat16 [8192, 1024], P(('groups', 'ctx'), 'kvh'), parts along dimension 0, may hold values from -4 to 4
- context_values: bfloat16 [8192, 1024], P(('groups', 'ctx'), 'kvh'), parts along dimension 0, may hold values from -16 to 16
- query_queries: bfloat16 [128, 8192], P(('groups', 'ctx'), ('kvh', 'rep')), parts along dimension 0, may hold values from -128 to 128
- query_keys: bfloat16 [128, 1024], P(('groups', 'ctx'), 'kvh'), parts along dimension 0, may hold values from -4 to 4
- query_values: bfloat16 [128, 1024], P(('groups', 'ctx'), 'kvh'), parts along dimension 0, may hold values from -4 to 4
Outputs:
- context_out: bfloat16 [8192, 8192], P(('groups', 'ctx'), ('kvh', 'rep')), parts along dimension 0
- query_out: bfloat16 [128, 8192], P(('groups', 'ctx'), ('kvh', 'rep')), parts along dimension 0
There are 2 independent parts, one for each index of `groups`. A program takes and returns all parts, laid end to end along the dimension named above; each array names one. Nothing has to cross between parts.
All inputs are finite; a program needn't handle non-finite values.
Results may differ from a plain program's by a relative error of at most 0.0026.
Values may be sent and summed in bfloat16 or wider, within the bound.
No kernel may reach another device: no remote copies, remote signals or barrier semaphores. Data moves between devices by JAX's collectives and lax.ppermute only.
A program may use at most 192 MiB of HBM per device.

v0:
```python
import math

import jax
import jax.numpy as jnp
from jax import lax
from jax.sharding import PartitionSpec as P

HD = 128


MASKED = -1e30


def broadcast(block, axis, owner):
    block = jnp.where(lax.axis_index(axis) == owner, block, jnp.zeros_like(block))
    return lax.psum(block, axis)


def merged_2(part, axis, combine):
    gathered = jax.tree.map(lambda a: lax.all_gather(a, axis), part)

    def take(source):
        return jax.tree.map(lambda a: lax.dynamic_index_in_dim(a, source, 0, False), gathered)

    return lax.fori_loop(
        1, lax.axis_size(axis), lambda source, state: combine(state, take(source)), take(0)
    )


def attend(query_tile, key_tile, value_tile, visible, scaling):
    scores = (
        jnp.einsum("qkgd,pkd->kgqp", query_tile, key_tile, preferred_element_type=jnp.float32)
        * scaling
    )
    scores = jnp.where(visible, scores, MASKED)
    maxima = jnp.max(scores, axis=-1)
    weights = jnp.exp(scores - maxima[..., None])
    totals = jnp.sum(weights, axis=-1)
    result = jnp.einsum(
        "kgqp,pkd->kgqd",
        weights.astype(jnp.bfloat16),
        value_tile,
        preferred_element_type=jnp.float32,
    )
    return (maxima, totals, result)


def combine(earlier, later):
    max_one, sum_one, out_one = earlier
    max_two, sum_two, out_two = later
    overall = jnp.maximum(max_one, max_two)
    factor_one = jnp.exp(max_one - overall)
    factor_two = jnp.exp(max_two - overall)
    return (
        overall,
        sum_one * factor_one + sum_two * factor_two,
        out_one * factor_one[..., None] + out_two * factor_two[..., None],
    )


def body(context_queries, context_keys, context_values, query_queries, query_keys, query_values):
    block_len = context_keys.shape[0]
    kv_device = context_keys.shape[1] // HD
    heads_device = context_queries.shape[1] // HD
    kv_used = max(kv_device // lax.axis_size("rep"), 1)
    group_device = heads_device // kv_used
    scaling = 1.0 / math.sqrt(HD)

    def select_heads(array):
        if kv_device > kv_used:
            return lax.dynamic_slice_in_dim(
                array, lax.axis_index("rep") * (kv_used * HD), kv_used * HD, 1
            )
        return array

    own_keys = select_heads(context_keys)
    own_values = select_heads(context_values)
    extra_keys = select_heads(query_keys)
    extra_values = select_heads(query_values)
    anchor = broadcast(jnp.stack([own_keys, own_values]), "ctx", 0)
    is_anchor = lax.axis_index("ctx") == 0
    key_rows = jnp.concatenate([anchor[0], own_keys], 0).reshape(2 * block_len, kv_used, HD)
    value_rows = jnp.concatenate([anchor[1], own_values], 0).reshape(2 * block_len, kv_used, HD)
    rows_per_tile = min(512, block_len)
    tile_count = block_len // rows_per_tile
    row_pos = jnp.arange(block_len, dtype=jnp.int32)
    columns = jnp.arange(2 * block_len, dtype=jnp.int32)
    visible_all = jnp.where(
        columns[None, :] < block_len,
        jnp.logical_not(is_anchor),
        columns[None, :] - block_len <= row_pos[:, None],
    )
    grouped_queries = context_queries.reshape(block_len, kv_used, group_device, HD)

    def one_tile(counter):
        row_start = counter * rows_per_tile
        query_tile = lax.dynamic_slice_in_dim(grouped_queries, row_start, rows_per_tile, 0)
        visible = lax.dynamic_slice_in_dim(visible_all, row_start, rows_per_tile, 0)
        maxima, totals, result = attend(
            query_tile, key_rows, value_rows, visible[None, None], scaling
        )
        normalized = (result / totals[..., None]).astype(jnp.bfloat16)
        return normalized.transpose(2, 0, 1, 3).reshape(rows_per_tile, heads_device * HD)

    tile_out = lax.map(one_tile, jnp.arange(tile_count, dtype=jnp.int32))
    context_out = tile_out.reshape(block_len, heads_device * HD)
    all_queries = lax.all_gather(query_queries, "ctx", axis=0, tiled=True)
    query_count = all_queries.shape[0]
    query_share = query_keys.shape[0]
    query_start = lax.axis_index("ctx") * query_share
    final_keys = jnp.concatenate([own_keys, extra_keys], 0).reshape(
        block_len + query_share, kv_used, HD
    )
    final_values = jnp.concatenate([own_values, extra_values], 0).reshape(
        block_len + query_share, kv_used, HD
    )
    query_pos = jnp.arange(query_count, dtype=jnp.int32)
    final_columns = jnp.arange(block_len + query_share, dtype=jnp.int32)
    final_visible = (final_columns[None, :] < block_len) | (
        query_start + final_columns[None, :] - block_len <= query_pos[:, None]
    )
    grouped_final = all_queries.reshape(query_count, kv_used, group_device, HD)
    maxima_k, totals_k, outputs_k = attend(
        grouped_final, final_keys, final_values, final_visible[None, None], scaling
    )
    maxima_all = maxima_k.reshape(heads_device, query_count)
    totals_all = totals_k.reshape(heads_device, query_count)
    outputs_all = outputs_k.reshape(heads_device, query_count, HD)
    overall, summed, numerator = merged_2((maxima_all, totals_all, outputs_all), "ctx", combine)
    merged = numerator / summed[..., None]
    mine = lax.dynamic_slice_in_dim(merged, query_start, query_share, 1)
    query_out = mine.transpose(1, 0, 2).reshape(query_share, heads_device * HD).astype(jnp.bfloat16)
    return (context_out, query_out)


def solution(mesh):
    in_specs = (
        P(("groups", "ctx"), ("kvh", "rep")),
        P(("groups", "ctx"), "kvh"),
        P(("groups", "ctx"), "kvh"),
        P(("groups", "ctx"), ("kvh", "rep")),
        P(("groups", "ctx"), "kvh"),
        P(("groups", "ctx"), "kvh"),
    )
    out_specs = (P(("groups", "ctx"), ("kvh", "rep")), P(("groups", "ctx"), ("kvh", "rep")))
    return jax.shard_map(body, mesh=mesh, in_specs=in_specs, out_specs=out_specs, check_vma=False)
```

profile of v0, /device:TPU:12, one launch (start us, length us, event | category | flops | bytes accessed | tf_op | source)
XLA Modules:
  0.0 254.5 jit_solution(10367177343645304288)
XLA Ops:
  7.2 1.3 constant_dynamic-slice_fusion.4
  8.5 1.1 maximum_select_fusion
  10.0 15.8 %all_gather.12 = bf16[64,2048]{1,0:T(8,128)(2,1)S(1)} all-gather(bf16[16,2048]{1,0:T(8,128)(2,1)S(1)} %copy-done.5), channel_id=1, replica_groups=mesh['groups'=2,'ctx'=4,'kvh'=2,'rep'=2] {'ctx'}, dimensions={0}, use_global_device_ids=true | all-gather | bytes 327680 | tf_op jit(solution)/shard_map/all_gather | solution.py:107
  26.0 1.1 fusion.20
  27.1 2.1 copy-done
  29.3 1.9 fusion.23
  31.2 3.5 %fusion.22 = f32[2,8,64]{2,1,0:T(8,128)S(1)} fusion(f32[2,1040,64,8]{1,2,3,0:T(8,128)} %copy-done, f32[2,8,64]{2,1,0:T(8,128)S(1)} %get-tuple-element.276, pred[64,1040]{1,0:T(8,128)(4,1)S(1)} %fusion.30), kind=kLoop, calls=%fused_computation.34 | loop fusion | flops 3193856 | bytes 4334592 | tf_op jit(solution)/shard_map/reduce_sum | solution.py:38
  35.1 13.4 %all_gather.14 = f32[4,16,64]{2,1,0:T(8,128)S(1)} all-gather(f32[1,16,64]{2,1,0:T(8,128)S(1)} %bitcast.122), channel_id=1, replica_groups=mesh['groups'=2,'ctx'=4,'kvh'=2,'rep'=2] {'ctx'}, dimensions={0}, use_global_device_ids=true | all-gather | bytes 20480 | tf_op jit(solution)/shard_map/all_gather | solution.py:20
  49.7 13.2 %all_gather.13 = f32[4,16,64]{2,1,0:T(8,128)S(1)} all-gather(f32[1,16,64]{2,1,0:T(8,128)S(1)} %bitcast.121), channel_id=1, replica_groups=mesh['groups'=2,'ctx'=4,'kvh'=2,'rep'=2] {'ctx'}, dimensions={0}, use_global_device_ids=true | all-gather | bytes 20480 | tf_op jit(solution)/shard_map/all_gather | solution.py:20
  64.0 6.4 %copy.34 = bf16[1024,2048]{0,1:T(8,128)(2,1)} copy(bf16[1024,2048]{1,0:T(8,128)(2,1)} %param.10) | data formatting | bytes 8388608 | tf_op args[0]
  70.4 3.0 %fusion.19 = pred[1024,2048]{1,0:T(8,128)(4,1)} fusion(s32[2048]{0:T(1024)S(1)} %iota_add_fusion, pred[]{:T(512)S(6)} %not.3, pred[2048]{0:T(1024)(128)(4,1)S(1)} %iota_compare_fusion.3), kind=kLoop, calls=%fused_computation.28 | loop fusion | flops 4194304 | bytes 2107393 | tf_op jit(solution)/shard_map/jit(_where)/select_n | solution.py:88
  73.4 1.3 fusion.36
  75.0 1.3 copy.40
  76.7 162.1 %while.29 = (s32[]{:T(128)}, bf16[2,512,2048]{2,1,0:T(8,128)(2,1)}, s32[2]{0:T(128)S(1)}, pred[1024,2048]{1,0:T(8,128)(4,1)}, bf16[1024,2,8,128]{0,3,2,1:T(8,128...) while((s32[]{:T(128)}, bf16[2,512,2048]{2,1,0:T(8,128)(2,1)}, ...), condition=%wide.region_4.5_spmd, body=%wide.region_1.4_spmd.sunk | while | flops 8776564736 | bytes 221414064 | solution.py:105
  78.1 1.3 constant_dynamic-slice_fusion.7
  79.4 26.5 %bitcast_reduce_fusion.2 = (f32[2,8,512]{2,1,0:T(8,128)S(1)}, f32[2,512,8,2048]{3,1,2,0:T(8,128)}) fusion(pred[512,2048]{1,0:T(8,128)(4,1)S(1)} %constant_dynamic-slice_fusion.7, bf16[2048,2,128]{2,0,1:T(8,128)(2,1)} %get-tuple-element.407, bf16[1024,2,8,128]{0,3,2,1:T(8,128)(2,1)} %get-tuple-element.406, s32[]{:T(128)S(6)} %select_n.92), kind=kOutput, calls=%fused_computation.1.clone.1 | convolution fusion | flops 4345290752 | bytes 71335936 | tf_op jit(solution)/shard_map/while/body/eval_jaxpr/qkgd,pkd->kgqp/dot_general | solution.py:32
  106.0 21.5 %fusion.46 = f32[2,8,512]{2,1,0:T(8,128)S(1)} fusion(f32[2,512,8,2048]{3,1,2,0:T(8,128)} %get-tuple-element.367, f32[2,8,512]{2,1,0:T(8,128)S(1)} %get-tuple-element.368, pred[512,2048]{1,0:T(8,128)(4,1)S(1)} %constant_dynamic-slice_fusion.7), kind=kLoop, calls=%fused_computation.4.clone.1 | loop fusion | flops 67100672 | bytes 68222976 | tf_op jit(solution)/shard_map/while/body/eval_jaxpr/reduce_sum | solution.py:38
  127.5 26.1 %fusion.47 = bf16[512,2,8,128]{0,3,2,1:T(8,128)(2,1)} fusion(f32[2,512,8,2048]{3,1,2,0:T(8,128)} %get-tuple-element.367, f32[2,8,512]{2,1,0:T(8,128)S(1)} %get-tuple-element.368, pred[512,2048]{1,0:T(8,128)(4,1)S(1)} %constant_dynamic-slice_fusion.7, f32[512,2,8]{0,2,1:T(8,128)S(1)} %bitcast.118, bf16[2048,2,128]{0,2,1:T(8,128)(2,1)S(1)} %get-tuple-element.408), kind=kOutput, calls=%fused_computation.9.clone.1 | convolution fusion | flops 4364173312 | bytes 71368704 | tf_op jit(solution)/shard_map/while/body/eval_jaxpr/kgqp,pkd->kgqd/dot_general | solution.py:39
  153.6 2.9 %copy.72 = bf16[1,512,2048]{2,1,0:T(8,128)(2,1)S(1)} copy(bf16[1,512,2048]{1,2,0:T(8,128)(2,1)} %bitcast.107) | data formatting | bytes 4194304 | tf_op jit(solution)/shard_map/while/body/jit(dynamic_update_index_in_dim)/dynamic_update_slice | solution.py:105
  156.5 1.5 constant_dynamic-update-slice_fusion.2
  159.2 1.3 constant_dynamic-slice_fusion.7
  160.5 26.3 %bitcast_reduce_fusion.2 = (f32[2,8,512]{2,1,0:T(8,128)S(1)}, f32[2,512,8,2048]{3,1,2,0:T(8,128)}) fusion(pred[512,2048]{1,0:T(8,128)(4,1)S(1)} %constant_dynamic-slice_fusion.7, bf16[2048,2,128]{2,0,1:T(8,128)(2,1)} %get-tuple-element.407, bf16[1024,2,8,128]{0,3,2,1:T(8,128)(2,1)} %get-tuple-element.406, s32[]{:T(128)S(6)} %select_n.92), kind=kOutput, calls=%fused_computation.1.clone.1 | convolution fusion | flops 4345290752 | bytes 71335936 | tf_op jit(solution)/shard_map/while/body/eval_jaxpr/qkgd,pkd->kgqp/dot_general | solution.py:32
  186.8 21.5 %fusion.46 = f32[2,8,512]{2,1,0:T(8,128)S(1)} fusion(f32[2,512,8,2048]{3,1,2,0:T(8,128)} %get-tuple-element.367, f32[2,8,512]{2,1,0:T(8,128)S(1)} %get-tuple-element.368, pred[512,2048]{1,0:T(8,128)(4,1)S(1)} %constant_dynamic-slice_fusion.7), kind=kLoop, calls=%fused_computation.4.clone.1 | loop fusion | flops 67100672 | bytes 68222976 | tf_op jit(solution)/shard_map/while/body/eval_jaxpr/reduce_sum | solution.py:38
  208.3 26.1 %fusion.47 = bf16[512,2,8,128]{0,3,2,1:T(8,128)(2,1)} fusion(f32[2,512,8,2048]{3,1,2,0:T(8,128)} %get-tuple-element.367, f32[2,8,512]{2,1,0:T(8,128)S(1)} %get-tuple-element.368, pred[512,2048]{1,0:T(8,128)(4,1)S(1)} %constant_dynamic-slice_fusion.7, f32[512,2,8]{0,2,1:T(8,128)S(1)} %bitcast.118, bf16[2048,2,128]{0,2,1:T(8,128)(2,1)S(1)} %get-tuple-element.408), kind=kOutput, calls=%fused_computation.9.clone.1 | convolution fusion | flops 4364173312 | bytes 71368704 | tf_op jit(solution)/shard_map/while/body/eval_jaxpr/kgqp,pkd->kgqd/dot_general | solution.py:39
  234.4 2.9 %copy.72 = bf16[1,512,2048]{2,1,0:T(8,128)(2,1)S(1)} copy(bf16[1,512,2048]{1,2,0:T(8,128)(2,1)} %bitcast.107) | data formatting | bytes 4194304 | tf_op jit(solution)/shard_map/while/body/jit(dynamic_update_index_in_dim)/dynamic_update_slice | solution.py:105
  237.3 1.5 constant_dynamic-update-slice_fusion.2
  238.8 1.1 slice_bitcast_fusion
  239.9 6.9 %while.30 = (s32[]{:T(128)}, f32[16,64]{1,0:T(8,128)S(1)}, f32[16,64]{1,0:T(8,128)S(1)}, f32[16,64,128]{2,1,0:T(8,128)S(1)}, f32[4,16,64]{2,1,0:T(8,128)}, /*ind...) while((s32[]{:T(128)}, f32[16,64]{1,0:T(8,128)S(1)}, ...), condition=%wide.region_8.9_spmd, body=%wide.region_7.8_spmd.sunk | while | flops 399365 | bytes 1613975 | solution.py:25
  240.6 1.5 fusion.49
  242.9 1.5 fusion.49
  245.2 1.5 fusion.49
  246.9 0.7 copy_bitcast_fusion
  (48 shorter events, 7.5 us)
Async XLA Ops:
  7.2 2.6 %copy-start.7 = (bf16[16,512]{1,0:T(8,128)(2,1)S(1)}, bf16[16,512]{1,0:T(8,128)(2,1)}, u32[]{:S(2)}) copy-start(bf16[16,512]{1,0:T(8,128)(2,1)} %param.14) | copy-start | bytes 49156
  7.2 2.6 %copy-start.6 = (bf16[16,512]{1,0:T(8,128)(2,1)S(1)}, bf16[16,512]{1,0:T(8,128)(2,1)}, u32[]{:S(2)}) copy-start(bf16[16,512]{1,0:T(8,128)(2,1)} %param.15) | copy-start | bytes 49156
  7.2 2.8 %copy-start.5 = (bf16[16,2048]{1,0:T(8,128)(2,1)S(1)}, bf16[16,2048]{1,0:T(8,128)(2,1)}, u32[]{:S(2)}) copy-start(bf16[16,2048]{1,0:T(8,128)(2,1)} %param.13) | copy-start | bytes 196612
  7.2 66.2 %all-reduce.2.cloned.1.call-start = ((), (), s32[]{:S(2)}) async-start(), calls=%async_computation | async-start | bytes 2097152 | tf_op jit(solution)/shard_map/psum | solution.py:16
  9.7 229.1 %all-gather.2.cloned.1.call-start = ((), (), s32[]{:S(2)}) async-start(), calls=%async_computation.1 | async-start | bytes 2621440 | tf_op jit(solution)/shard_map/all_gather | solution.py:20
  27.1 2.1 copy-start
  48.5 0.6 copy-start.3
  62.8 0.6 copy-start.4
  76.6 163.2 %copy-start.1 = (f32[16,64]{1,0:T(8,128)S(1)}, f32[16,64]{1,0:T(8,128)}, u32[]{:S(2)}) copy-start(f32[16,64]{1,0:T(8,128)} %slice_bitcast_fusion.1) | copy-start | bytes 12292
  76.7 163.2 %copy-start.2 = (f32[16,64]{1,0:T(8,128)S(1)}, f32[16,64]{1,0:T(8,128)}, u32[]{:S(2)}) copy-start(f32[16,64]{1,0:T(8,128)} %slice_bitcast_fusion.2) | copy-start | bytes 12292
Sparse Core Ops, SparseCore 0:
  10.4 55.3 all-reduce.1
  67.5 43.9 all-gather.1
where the time goes:
time: 257 us; the launch traced here: 254 us
  matrix products  108 us (42%)
  other arithmetic  58.4 us (23%)
  blocking collectives  42.3 us (16%)
  local copies, waits for them, and re-layouts  29.8 us (12%)
  between operations  14.3 us (6%)
    dot_general x3, matrix products, attend(): jnp.einsum('kgqp,pkd->kgqd', weights.astype(jnp.bfloat16), value_tile, pr...  54 us
    dot_general x3, matrix products, attend(): jnp.einsum('qkgd,pkd->kgqp', query_tile, key_tile, preferred_element_type...  53.9 us
    reduce_sum x3, other arithmetic, attend(): totals = jnp.sum(weights, axis=-1)  46.5 us
    all_gather x2, blocking collectives, merged_2(): gathered = jax.tree.map(lambda a: lax.all_gather(a, axis), part)  26.5 us
    all_gather x1, blocking collectives, body(): all_queries = lax.all_gather(query_queries, 'ctx', axis=0, tiled=True)  15.8 us
    unnamed x18, local copies, waits for them, and re-layouts  9.8 us
    dynamic_update_slice x4, local copies, waits for them, and re-layouts, body(): tile_out = lax.map(one_tile, jnp.arange(tile_count, dtype=jnp.int32))  8.77 us
  transfers between devices with their start and end apart: 2, of which 0 were waited for; matrix products, arithmetic and copies ran while one was open for 71% of the time, Pallas kernels for 0%

commit v1 on v0

v1 whole, which is shorter than its diff:
```python
import functools
import math

import jax
import jax.numpy as jnp
from jax import lax
from jax.experimental import pallas as pl
from jax.experimental.pallas import tpu as pltpu
from jax.sharding import PartitionSpec as P

HD = 128
MASKED = -1e30
SCALE = math.log2(math.e) / math.sqrt(HD)
SAFE = 2.0**100
F32 = jnp.float32
BF16 = jnp.bfloat16
NT = (((1,), (1,)), ((), ()))
NN = (((1,), (0,)), ((), ()))
VMEM_LIMIT = 56 * 2**20


def dot(a, b, dims):
    return lax.dot_general(a, b, dims, preferred_element_type=F32)


def tile_of(length):
    return math.gcd(length, 256)


def own_kernel(off_ref, q_ref, k_ref, v_ref, acc_ref, stat_ref, *, heads):
    rows = q_ref.shape[0]
    tile = tile_of(rows)
    values = v_ref[...].T
    jobs = [(h, i) for h in range(heads) for i in range(rows // tile)]
    causal = lax.broadcasted_iota(jnp.int32, (tile, tile), 0) <= lax.broadcasted_iota(
        jnp.int32, (tile, tile), 1
    )

    def score(job):
        h, i = job
        q = q_ref[i * tile : (i + 1) * tile, h * HD : (h + 1) * HD]
        s = dot(k_ref[: (i + 1) * tile, :], q, NT)
        last = jnp.where(causal, s[i * tile :], MASKED)
        return last if i == 0 else jnp.concatenate([s[: i * tile], last], 0)

    def soften(s):
        top = jnp.max(s, 0, keepdims=True) * SCALE
        p = jnp.exp2(s * SCALE - top)
        return p.astype(BF16), top, jnp.sum(p, 0, keepdims=True)

    def finish(job, state):
        h, i = job
        p, top, total = state
        columns = slice(i * tile, (i + 1) * tile)
        acc_ref[h, :, columns] = dot(values[:, : (i + 1) * tile], p, NN)
        stat_ref[h, 0:1, columns] = top
        stat_ref[h, 1:2, columns] = total

    scores, weights = {0: score(jobs[0])}, {}
    for t in range(len(jobs) + 1):
        if t + 1 < len(jobs):
            scores[t + 1] = score(jobs[t + 1])
        if t < len(jobs):
            weights[t] = soften(scores.pop(t))
        if t > 0:
            finish(jobs[t - 1], weights.pop(t - 1))


def anchor_kernel(pos_ref, q_ref, acc_ref, stat_ref, *refs, heads, parts):
    part_refs, (o_ref, k_ref, vt_ref) = refs[:parts], refs[-3:]
    rows = q_ref.shape[0]
    tile = tile_of(rows)
    size = part_refs[0].shape[1]
    jobs = [(h, i) for h in range(heads) for i in range(rows // tile)]

    def query(h, i):
        return q_ref[i * tile : (i + 1) * tile, h * HD : (h + 1) * HD]

    @pl.when(pos_ref[0] == 0)
    def _():
        for h, i in jobs:
            columns = slice(i * tile, (i + 1) * tile)
            out = acc_ref[h, :, columns] / stat_ref[h, 1:2, columns]
            o_ref[columns, h * HD : (h + 1) * HD] = out.T.astype(BF16)

    @pl.when(pos_ref[0] > 0)
    def _():
        @pl.when(pl.program_id(0) == 0)
        def _():
            def assemble(v_ref):
                for r in range(parts):
                    start = pl.multiple_of(pos_ref[1 + r], 16)
                    k_ref[pl.ds(start, size), :] = part_refs[r][0]
                    v_ref[pl.ds(start, size), :] = part_refs[r][1]
                vt_ref[...] = v_ref[...].T

            pl.run_scoped(assemble, pltpu.VMEM(k_ref.shape, BF16))

        largest = None
        for h, i in jobs:
            columns = slice(i * tile, (i + 1) * tile)
            s = dot(k_ref[...], query(h, i), NT)
            p = jnp.exp2(s * SCALE - stat_ref[h, 0:1, columns])
            total = stat_ref[h, 1:2, columns] + jnp.sum(p, 0, keepdims=True)
            out = acc_ref[h, :, columns] + dot(vt_ref[...], p.astype(BF16), NN)
            o_ref[columns, h * HD : (h + 1) * HD] = (out / total).T.astype(BF16)
            worst = jnp.where(total < SAFE, 0.0, 1.0)
            largest = worst if largest is None else jnp.maximum(largest, worst)

        @pl.when(jnp.max(largest) > 0.0)
        def _():
            for h in range(heads):

                @pl.loop(0, rows // tile)
                def _(i):
                    columns = pl.ds(pl.multiple_of(i * tile, tile), tile)
                    s = dot(k_ref[...], q_ref[columns, h * HD : (h + 1) * HD], NT) * SCALE
                    own_top = stat_ref[h, 0:1, columns]
                    top = jnp.maximum(own_top, jnp.max(s, 0, keepdims=True))
                    p = jnp.exp2(s - top)
                    factor = jnp.exp2(own_top - top)
                    total = stat_ref[h, 1:2, columns] * factor + jnp.sum(p, 0, keepdims=True)
                    out = acc_ref[h, :, columns] * factor + dot(vt_ref[...], p.astype(BF16), NN)
                    o_ref[columns, h * HD : (h + 1) * HD] = (out / total).T.astype(BF16)


def partial_kernel(pos_ref, *refs, shares, kv, group):
    q_refs, (k_ref, v_ref, xk_ref, xv_ref, out_ref) = refs[:shares], refs[shares:]
    share = xk_ref.shape[0]
    width = group * share
    mine = pos_ref[0]
    row = lax.broadcasted_iota(jnp.int32, (share, width), 0)
    column = lax.broadcasted_iota(jnp.int32, (share, width), 1) % share
    for g in range(kv):
        lanes = slice(g * HD, (g + 1) * HD)
        keys, extra = k_ref[:, lanes], xk_ref[:, lanes]
        values, extra_values = v_ref[:, lanes].T, xv_ref[:, lanes].T
        for r in range(shares):
            source = lax.rem(mine - r + shares, shares)
            q = jnp.concatenate(
                [q_refs[r][:, (g * group + h) * HD : (g * group + h + 1) * HD] for h in range(group)], 0
            )
            s = dot(keys, q, NT)
            x = jnp.where(mine * share + row <= source * share + column, dot(extra, q, NT), MASKED)
            top = jnp.maximum(jnp.max(s, 0, keepdims=True), jnp.max(x, 0, keepdims=True)) * SCALE
            p, px = jnp.exp2(s * SCALE - top), jnp.exp2(x * SCALE - top)
            total = jnp.sum(p, 0, keepdims=True) + jnp.sum(px, 0, keepdims=True)
            acc = dot(values, p.astype(BF16), NN) + dot(extra_values, px.astype(BF16), NN)
            out_ref[r, g * width : (g + 1) * width, :] = acc.T
            out_ref[r, kv * width + 2 * g : kv * width + 2 * g + 1, :width] = top
            out_ref[r, kv * width + 2 * g + 1 : kv * width + 2 * g + 2, :width] = total


def merge_kernel(*refs, shares, kv, group):
    part_refs, out_ref = refs[:shares], refs[shares]
    share = out_ref.shape[0]
    width = group * share
    for g in range(kv):
        at = kv * width + 2 * g
        tops = [ref[0, at : at + 1, :width] for ref in part_refs]
        overall = functools.reduce(jnp.maximum, tops)
        factors = [jnp.exp2(top - overall) for top in tops]
        summed = sum(f * ref[0, at + 1 : at + 2, :width] for f, ref in zip(factors, part_refs))
        out = sum(
            f.reshape(width, 1) * ref[0, g * width : (g + 1) * width, :]
            for f, ref in zip(factors, part_refs)
        )
        out = (out / summed.reshape(width, 1)).astype(BF16)
        for h in range(group):
            out_ref[:, (g * group + h) * HD : (g * group + h + 1) * HD] = out[h * share : (h + 1) * share]


def body(context_queries, context_keys, context_values, query_queries, query_keys, query_values):
    rows = context_keys.shape[0]
    kv_device = context_keys.shape[1] // HD
    heads = context_queries.shape[1] // HD
    kv = max(kv_device // lax.axis_size("rep"), 1)
    group = heads // kv
    share = query_keys.shape[0]
    blocks = lax.axis_size("ctx")
    mine = lax.axis_index("ctx")
    offset = lax.axis_index("rep") * kv if kv_device > kv else jnp.int32(0)
    params = pltpu.CompilerParams(vmem_limit_bytes=VMEM_LIMIT)
    at_once = math.gcd(group, 4)

    parts = blocks - 1
    size = min(-(-rows // parts // 16) * 16, rows)
    starts = [min(r * size, rows - size) for r in range(parts)]

    def scatter(g):
        got = None
        for r in range(parts):
            piece = jnp.stack(
                [
                    lax.dynamic_slice(a, (starts[r], (offset + g) * HD), (size, HD))
                    for a in (context_keys, context_values)
                ]
            )
            sent = lax.ppermute(piece, "ctx", [(0, r + 1)])
            got = sent if got is None else jnp.where(mine == r + 1, sent, got)
        return got

    def exchange(part):
        return [part] + [
            lax.ppermute(part, "ctx", [(z + 1, (z + d) % parts + 1) for z in range(parts)])
            for d in range(1, parts)
        ]

    slot_part = [lax.rem(mine - 1 - d + 2 * parts, parts) for d in range(parts)]
    position = jnp.stack(
        [mine] + [jnp.minimum(part * size, rows - size) for part in slot_part]
    ).astype(jnp.int32)

    others = [
        lax.ppermute(query_queries, "ctx", [(z, (z + r) % blocks) for z in range(blocks)])
        for r in range(1, blocks)
    ]
    own_part = [scatter(g) for g in range(kv)]

    own_cost = pl.CostEstimate(
        flops=3 * heads * rows * rows * HD, bytes_accessed=8 * rows * heads * HD, transcendentals=0
    )
    per_kv = group // at_once
    acc, stats = pl.pallas_call(
        functools.partial(own_kernel, heads=at_once),
        grid_spec=pltpu.PrefetchScalarGridSpec(
            num_scalar_prefetch=1,
            grid=(heads // at_once,),
            in_specs=[
                pl.BlockSpec((rows, at_once * HD), lambda j, off: (0, j)),
                pl.BlockSpec((rows, HD), lambda j, off: (0, off[0] + j // per_kv)),
                pl.BlockSpec((rows, HD), lambda j, off: (0, off[0] + j // per_kv)),
            ],
            out_specs=[
                pl.BlockSpec((at_once, HD, rows), lambda j, off: (j, 0, 0)),
                pl.BlockSpec((at_once, 2, rows), lambda j, off: (j, 0, 0)),
            ],
        ),
        out_shape=[
            jax.ShapeDtypeStruct((heads, HD, rows), F32),
            jax.ShapeDtypeStruct((heads, 2, rows), F32),
        ],
        compiler_params=params,
        cost_estimate=own_cost,
        name="own",
    )(offset.reshape(1), context_queries, context_keys, context_values)

    pieces = [exchange(part) for part in own_part]

    payload_rows = -(-(kv * group * share + 2 * kv) // 8) * 8
    partial = pl.pallas_call(
        functools.partial(partial_kernel, shares=blocks, kv=kv, group=group),
        grid_spec=pltpu.PrefetchScalarGridSpec(
            num_scalar_prefetch=1,
            grid=(1,),
            in_specs=[pl.BlockSpec((share, heads * HD), lambda j, pos: (0, 0))] * blocks
            + [pl.BlockSpec((rows, kv * HD), lambda j, pos: (0, pos[1]))] * 2
            + [pl.BlockSpec((share, kv * HD), lambda j, pos: (0, pos[1]))] * 2,
            out_specs=pl.BlockSpec((blocks, payload_rows, HD), lambda j, pos: (0, 0, 0)),
        ),
        out_shape=jax.ShapeDtypeStruct((blocks, payload_rows, HD), F32),
        compiler_params=params,
        name="partial",
    )(
        jnp.stack([mine, offset // kv]).astype(jnp.int32),
        query_queries,
        *others,
        context_keys,
        context_values,
        query_keys,
        query_values,
    )
    returned = [partial[0:1]] + [
        lax.ppermute(partial[r : r + 1], "ctx", [(z, (z - r) % blocks) for z in range(blocks)])
        for r in range(1, blocks)
    ]

    context_out = None
    for g in range(kv):
        first = g * per_kv
        operands = [position, context_queries, acc, stats, *pieces[g]]
        in_specs = [
            pl.BlockSpec((rows, at_once * HD), lambda j, pos, first=first: (0, first + j)),
            pl.BlockSpec((at_once, HD, rows), lambda j, pos, first=first: (first + j, 0, 0)),
            pl.BlockSpec((at_once, 2, rows), lambda j, pos, first=first: (first + j, 0, 0)),
        ] + [pl.BlockSpec((2, size, HD), lambda j, pos: (0, 0, 0))] * parts
        if context_out is not None:
            operands.append(context_out)
            in_specs.append(pl.BlockSpec(memory_space=pl.ANY))
        context_out = pl.pallas_call(
            functools.partial(anchor_kernel, heads=at_once, parts=parts),
            grid_spec=pltpu.PrefetchScalarGridSpec(
                num_scalar_prefetch=1,
                grid=(per_kv,),
                in_specs=in_specs,
                out_specs=pl.BlockSpec(
                    (rows, at_once * HD), lambda j, pos, first=first: (0, first + j)
                ),
                scratch_shapes=[pltpu.VMEM((rows, HD), BF16), pltpu.VMEM((HD, rows), BF16)],
            ),
            out_shape=jax.ShapeDtypeStruct((rows, heads * HD), BF16),
            input_output_aliases={} if context_out is None else {len(operands) - 1: 0},
            compiler_params=params,
            cost_estimate=pl.CostEstimate(
                flops=4 * group * rows * rows * HD,
                bytes_accessed=8 * rows * group * HD,
                transcendentals=0,
            ),
            name="anchor",
        )(*operands)

    query_out = pl.pallas_call(
        functools.partial(merge_kernel, shares=blocks, kv=kv, group=group),
        out_shape=jax.ShapeDtypeStruct((share, heads * HD), BF16),
        compiler_params=params,
        name="merge",
    )(*returned)
    return context_out, query_out


def solution(mesh):
    in_specs = (
        P(("groups", "ctx"), ("kvh", "rep")),
        P(("groups", "ctx"), "kvh"),
        P(("groups", "ctx"), "kvh"),
        P(("groups", "ctx"), ("kvh", "rep")),
        P(("groups", "ctx"), "kvh"),
        P(("groups", "ctx"), "kvh"),
    )
    out_specs = (P(("groups", "ctx"), ("kvh", "rep")), P(("groups", "ctx"), ("kvh", "rep")))
    return jax.shard_map(body, mesh=mesh, in_specs=in_specs, out_specs=out_specs, check_vma=False)
```

time: 257 us -> 108 us (0.42)
  matrix products: 108 us -> 0 us
  Pallas kernels: 0 us -> 64.5 us
  other arithmetic: 58.4 us -> 1.38 us
  blocking collectives: 42.3 us -> 0 us
  starting transfers between devices: 0.08 us -> 30.2 us
  local copies, waits for them, and re-layouts: 29.8 us -> 5.87 us
  between operations: 14.3 us -> 1.02 us
  waiting for transfers between devices: 0.04 us -> 4.36 us
    dot_general x6 -> x0, matrix products: 108 us -> none  [the longest x3 54 us: attend(): jnp.einsum('kgqp,pkd->kgqd', weights.astype(jnp.bfloat16), value_tile, pr...]
    pallas_call x0 -> x5, Pallas kernels: none -> 64.5 us  [the longest x2 38.3 us: body(): pl.pallas_call(functools.partial(anchor_kernel, heads=at_once, parts=part...]
    reduce_sum x3 -> x0, other arithmetic: 46.5 us -> none  [attend(): totals = jnp.sum(weights, axis=-1)]
    all_gather x3 -> x0, blocking collectives: 42.3 us -> none  [the longest x2 26.5 us: merged_2(): gathered = jax.tree.map(lambda a: lax.all_gather(a, axis), part)]
    ppermute x0 -> x16, starting transfers between devices: none -> 30.2 us  [the longest x4 13.7 us: exchange(): lax.ppermute(part, 'ctx', [(z + 1, (z + d) % parts + 1) for z in range(pa...]
    dynamic_update_slice x4 -> x0, local copies, waits for them, and re-layouts: 8.77 us -> none  [body(): tile_out = lax.map(one_tile, jnp.arange(tile_count, dtype=jnp.int32))]
    unnamed x18 -> x24, local copies, waits for them, and re-layouts: 9.8 us -> 2.68 us
    add x6 -> x0, other arithmetic: 6.84 us -> none  [the longest x3 4.65 us: combine(): out_one * factor_one[..., None] + out_two * factor_two[..., None]]
  transfers between devices with their start and end apart: 2 -> 16, of which waited for: 0 -> 1; matrix products, arithmetic and copies ran while one was open for 71% -> 4% of each run, Pallas kernels for 0% -> 42%
where the time goes in v1:
time: 108 us; the launch traced here: 107 us
  Pallas kernels  64.5 us (60%)
  starting transfers between devices  30.2 us (28%)
  local copies, waits for them, and re-layouts  5.87 us (5%)
  waiting for transfers between devices  4.36 us (4%)
  other arithmetic  1.38 us (1%)
    pallas_call x2, Pallas kernels, body(): pl.pallas_call(functools.partial(anchor_kernel, heads=at_once, parts=part...  38.3 us
    pallas_call x1, Pallas kernels, body(): pl.pallas_call(functools.partial(own_kernel, heads=at_once), grid_spec=pl...  17.1 us
    ppermute x4, starting transfers between devices, exchange(): lax.ppermute(part, 'ctx', [(z + 1, (z + d) % parts + 1) for z in range(pa...  13.7 us
    pallas_call x1, Pallas kernels, body(): pl.pallas_call(functools.partial(partial_kernel, shares=blocks, kv=kv, gr...  7.12 us
    ppermute x3, starting transfers between devices, body(): lax.ppermute(partial[r:r + 1], 'ctx', [(z, (z - r) % blocks) for z in ran...  6.6 us
    ppermute x6, starting transfers between devices, scatter(): sent = lax.ppermute(piece, 'ctx', [(0, r + 1)])  5.25 us
    ppermute x3, starting transfers between devices, body(): lax.ppermute(query_queries, 'ctx', [(z, (z + r) % blocks) for z in range(...  4.67 us
    ppermute x4, waiting for transfers between devices, exchange(): lax.ppermute(part, 'ctx', [(z + 1, (z + d) % parts + 1) for z in range(pa...  4.32 us
  transfers between devices with their start and end apart: 16, of which 1 were waited for; matrix products, arithmetic and copies ran while one was open for 4% of the time, Pallas kernels for 42%

profile of v1, /device:TPU:12, one launch (start us, length us, event | category | flops | bytes accessed | tf_op | source)
XLA Modules:
  0.0 107.3 jit_solution(16071740626762415491)
XLA Ops:
  0.6 1.6 %collective-permute-start.10 = (bf16[16,2048]{1,0:T(8,128)(2,1)}, bf16[16,2048]{1,0:T(8,128)(2,1)S(1)}, u32[]{:S(2)}, u32[]{:S(2)}) collective-permute-start(bf16[16,2048]{1,0:T(8,128)(2,1)} %refs_0_.1), channel_id=1, source_target_pairs={{0,4},{4,8},{8,12},{12,0},{1,5},{5,9},{9,13},{13,1},{2,6},{6,10},{... | collective-permute-start | bytes 196616 | tf_op jit(solution)/shard_map/ppermute | solution.py:215
  2.3 1.2 %collective-permute-start.11 = (bf16[16,2048]{1,0:T(8,128)(2,1)}, bf16[16,2048]{1,0:T(8,128)(2,1)S(1)}, u32[]{:S(2)}, u32[]{:S(2)}) collective-permute-start(bf16[16,2048]{1,0:T(8,128)(2,1)} %refs_0_.1), channel_id=1, source_target_pairs={{0,8},{4,12},{8,0},{12,4},{1,9},{5,13},{9,1},{13,5},{2,10},{6,14},... | collective-permute-start | bytes 196616 | tf_op jit(solution)/shard_map/ppermute | solution.py:215
  3.5 1.8 %collective-permute-start.12 = (bf16[16,2048]{1,0:T(8,128)(2,1)}, bf16[16,2048]{1,0:T(8,128)(2,1)S(1)}, u32[]{:S(2)}, u32[]{:S(2)}) collective-permute-start(bf16[16,2048]{1,0:T(8,128)(2,1)} %refs_0_.1), channel_id=1, source_target_pairs={{0,12},{4,0},{8,4},{12,8},{1,13},{5,1},{9,5},{13,9},{2,14},{6,2},{... | collective-permute-start | bytes 196616 | tf_op jit(solution)/shard_map/ppermute | solution.py:215
  5.3 1.4 %dynamic-slice_bitcast_fusion = (bf16[1,352,128]{2,1,0:T(8,128)(2,1)S(1)}, bf16[1,352,128]{2,1,0:T(8,128)(2,1)S(1)}, bf16[1,352,128]{2,1,0:T(8,128)(2,1)S(1)}, b...) fusion(bf16[1024,512]{1,0:T(8,128)(2,1)} %refs_5_.1, ...), kind=kLoop, calls=%fused_computation.8 | loop fusion | bytes 2162696 | tf_op jit(solution)/shard_map/stack | solution.py:193
  6.7 0.7 collective-permute-start.5
  7.4 0.7 collective-permute-start.6
  8.2 17.1 %own.1 = (f32[16,128,1024]{2,1,0:T(8,128)}, f32[16,2,1024]{2,1,0:T(2,128)}) custom-call(s32[1]{0:T(128)} %bitcast.4.off_ref, bf16[1024,2048]{1,0:T(8,128)(2,1)} %q_ref.5, bf16[1024,512]{1,0:T(8,128)(2,1)} %refs_4_.1, bf16[1024,512]{1,0:T(8,128)(2,1)} %refs_5_.1), custom_call_target="tpu_custom_call" | custom-call | flops 6442450944 | bytes 16777216 | tf_op jit(solution)/shard_map/own/pallas_call | solution.py:224
  25.4 0.6 pad_add_fusion.1.pos_ref
  26.0 0.6 pad_add_fusion.pos_ref
  26.6 1.3 %collective-permute-start.7 = (bf16[2,352,128]{2,1,0:T(8,128)(2,1)S(1)}, bf16[2,352,128]{2,1,0:T(8,128)(2,1)S(1)}, u32[]{:S(2)}, u32[]{:S(2)}) collective-permute-start(bf16[2,352,128]{2,1,0:T(8,128)(2,1)S(1)} %pad_maximum_fusion.5), channel_id=1, source_target_pairs={{0,4},{1,5},{2,6},{3,7},{16,20},{17,21},{18,22},{19,23}} | collective-permute-start | bytes 540680 | tf_op jit(solution)/shard_map/ppermute | solution.py:199
  27.9 0.0 collective-permute-done.11.refs_2_
  27.9 0.7 collective-permute-start
  28.6 0.0 collective-permute-done.12.refs_3_
  28.6 0.7 collective-permute-start.1
  29.4 7.1 %partial.1 = f32[4,264,128]{2,1,0:T(8,128)} custom-call(s32[2]{0:T(128)} %pad_add_fusion.1.pos_ref, bf16[16,2048]{1,0:T(8,128)(2,1)} %refs_0_.1, bf16[16,2048]{1,0:T(8,128)(2,1)} %copy-done.9, bf16[16,2048]{1,0:T(8,128)(2,1)} %copy-done.10, bf16[16,2048]{1,0:T(8,128)(2,1)} %copy-done.11, bf16[1024,512]{1,0:T(8,128)(2,1)} %refs_4_.1, ...), custom_call_target="tpu_custom_call" | custom-call | tf_op jit(solution)/shard_map/partial/pallas_call | solution.py:251
  36.5 1.8 %fusion = (f32[1,264,128]{2,1,0:T(8,128)S(1)}, f32[1,264,128]{2,1,0:T(8,128)S(1)}, f32[1,264,128]{2,1,0:T(8,128)S(1)}, f32[1,264,128]{2,1,0:T(8,128)}) fusion(f32[4,264,128]{2,1,0:T(8,128)} %partial.1), kind=kLoop, calls=%fused_computation.22 | loop fusion | bytes 1081344 | tf_op jit(solution)/shard_map/slice | solution.py:274
  38.3 1.3 %collective-permute-start.2 = (bf16[2,352,128]{2,1,0:T(8,128)(2,1)S(1)}, bf16[2,352,128]{2,1,0:T(8,128)(2,1)S(1)}, u32[]{:S(2)}, u32[]{:S(2)}) collective-permute-start(bf16[2,352,128]{2,1,0:T(8,128)(2,1)S(1)} %pad_maximum_fusion.2), channel_id=1, source_target_pairs={{0,4},{1,5},{2,6},{3,7},{16,20},{17,21},{18,22},{19,23}} | collective-permute-start | bytes 540680 | tf_op jit(solution)/shard_map/ppermute | solution.py:199
  39.6 5.0 %collective-permute-start.13 = (f32[1,264,128]{2,1,0:T(8,128)S(1)}, f32[1,264,128]{2,1,0:T(8,128)S(1)}, u32[]{:S(2)}, u32[]{:S(2)}) collective-permute-start(f32[1,264,128]{2,1,0:T(8,128)S(1)} %get-tuple-element.20), channel_id=1, source_target_pairs={{0,12},{4,0},{8,4},{12,8},{1,13},{5,1},{9,5},{13,9},{2,14},{6,2},{... | collective-permute-start | bytes 405512 | tf_op jit(solution)/shard_map/ppermute | solution.py:274
  44.6 1.6 %collective-permute-start.15 = (f32[1,264,128]{2,1,0:T(8,128)S(1)}, f32[1,264,128]{2,1,0:T(8,128)S(1)}, u32[]{:S(2)}, u32[]{:S(2)}) collective-permute-start(f32[1,264,128]{2,1,0:T(8,128)S(1)} %get-tuple-element.18), channel_id=1, source_target_pairs={{0,4},{4,8},{8,12},{12,0},{1,5},{5,9},{9,13},{13,1},{2,6},{6,10},{... | collective-permute-start | bytes 405512 | tf_op jit(solution)/shard_map/ppermute | solution.py:274
  46.2 3.8 %collective-permute-start.8 = (bf16[2,352,128]{2,1,0:T(8,128)(2,1)S(1)}, bf16[2,352,128]{2,1,0:T(8,128)(2,1)S(1)}, u32[]{:S(2)}, u32[]{:S(2)}) collective-permute-start(bf16[2,352,128]{2,1,0:T(8,128)(2,1)S(1)} %select_select_fusion.refs_0_), channel_id=1, source_target_pairs={{4,8},{8,12},{12,4},{5,9},{9,13},{13,5},{6,10},{10,14},{14,6},{7,1... | collective-permute-start | bytes 540680 | tf_op jit(solution)/shard_map/ppermute | solution.py:205
  50.1 2.9 %collective-permute-start.9 = (bf16[2,352,128]{2,1,0:T(8,128)(2,1)S(1)}, bf16[2,352,128]{2,1,0:T(8,128)(2,1)S(1)}, u32[]{:S(2)}, u32[]{:S(2)}) collective-permute-start(bf16[2,352,128]{2,1,0:T(8,128)(2,1)S(1)} %select_select_fusion.refs_0_), channel_id=1, source_target_pairs={{4,12},{8,4},{12,8},{5,13},{9,5},{13,9},{6,14},{10,6},{14,10},{7,1... | collective-permute-start | bytes 540680 | tf_op jit(solution)/shard_map/ppermute | solution.py:205
  53.0 0.0 copy-start.6
  53.0 3.0 %collective-permute-start.3 = (bf16[2,352,128]{2,1,0:T(8,128)(2,1)S(1)}, bf16[2,352,128]{2,1,0:T(8,128)(2,1)S(1)}, u32[]{:S(2)}, u32[]{:S(2)}) collective-permute-start(bf16[2,352,128]{2,1,0:T(8,128)(2,1)S(1)} %select_select_fusion.1.refs_0_), channel_id=1, source_target_pairs={{4,8},{8,12},{12,4},{5,9},{9,13},{13,5},{6,10},{10,14},{14,6},{7,1... | collective-permute-start | bytes 540680 | tf_op jit(solution)/shard_map/ppermute | solution.py:205
  56.0 4.0 %collective-permute-start.4 = (bf16[2,352,128]{2,1,0:T(8,128)(2,1)S(1)}, bf16[2,352,128]{2,1,0:T(8,128)(2,1)S(1)}, u32[]{:S(2)}, u32[]{:S(2)}) collective-permute-start(bf16[2,352,128]{2,1,0:T(8,128)(2,1)S(1)} %select_select_fusion.1.refs_0_), channel_id=1, source_target_pairs={{4,12},{8,4},{12,8},{5,13},{9,5},{13,9},{6,14},{10,6},{14,10},{7,1... | collective-permute-start | bytes 540680 | tf_op jit(solution)/shard_map/ppermute | solution.py:205
  60.0 0.6 copy-done.8
  60.7 2.0 %merge.1 = bf16[16,2048]{1,0:T(8,128)(2,1)} custom-call(f32[1,264,128]{2,1,0:T(8,128)} %get-tuple-element.21.refs_0_, f32[1,264,128]{2,1,0:T(8,128)} %copy-done.6, f32[1,264,128]{2,1,0:T(8,128)} %copy-done.7, f32[1,264,128]{2,1,0:T(8,128)} %copy-done.8), custom_call_target="tpu_custom_call" | custom-call | tf_op jit(solution)/shard_map/merge/pallas_call | solution.py:312
  62.7 4.3 %collective-permute-done.9.refs_2_ = bf16[2,352,128]{2,1,0:T(8,128)(2,1)S(1)} collective-permute-done((bf16[2,352,128]{2,1,0:T(8,128)(2,1)S(1)}, bf16[2,352,128]{2,1,0:T(8,128)(2,1)S(1)}, u32[]{:S(2)}, u32[]{:S(2)}) %collective-permute-start.9) | collective-permute-done | bytes 180256 | tf_op jit(solution)/shard_map/ppermute | solution.py:205
  67.0 0.7 copy-done.3
  67.7 19.0 %anchor.2.refs_3_ = bf16[1024,2048]{1,0:T(8,128)(2,1)} custom-call(s32[4]{0:T(128)} %pad_add_fusion.pos_ref, bf16[1024,2048]{1,0:T(8,128)(2,1)} %q_ref.5, f32[16,128,1024]{2,1,0:T(8,128)} %get-tuple-element.4.acc_ref, f32[16,2,1024]{2,1,0:T(2,128)} %get-tuple-element.5.stat_ref, bf16[2,352,128]{2,1,0:T(8,128)(2,1)} %copy-done, ...), custom_call_target="tpu_custom_call" | custom-call | flops 4294967296 | bytes 8388608 | tf_op jit(solution)/shard_map/anchor/pallas_call | solution.py:290
  86.7 0.7 copy-done.4
  87.4 0.7 copy-done.5
  88.1 19.3 %anchor.3 = bf16[1024,2048]{1,0:T(8,128)(2,1)} custom-call(s32[4]{0:T(128)} %pad_add_fusion.pos_ref, bf16[1024,2048]{1,0:T(8,128)(2,1)} %q_ref.5, f32[16,128,1024]{2,1,0:T(8,128)} %get-tuple-element.4.acc_ref, f32[16,2,1024]{2,1,0:T(2,128)} %get-tuple-element.5.stat_ref, bf16[2,352,128]{2,1,0:T(8,128)(2,1)} %copy-done.1, ...), custom_call_target="tpu_custom_call", output_to_operand_aliasing={{}: (7, {})} | custom-call | flops 4294967296 | bytes 8388608 | tf_op jit(solution)/shard_map/anchor/pallas_call | solution.py:290
  (41 shorter events, 0.2 us)
Async XLA Ops:
  0.6 26.0 %collective-permute-start.10 = (bf16[16,2048]{1,0:T(8,128)(2,1)}, bf16[16,2048]{1,0:T(8,128)(2,1)S(1)}, u32[]{:S(2)}, u32[]{:S(2)}) collective-permute-start(bf16[16,2048]{1,0:T(8,128)(2,1)} %refs_0_.1), channel_id=1, source_target_pairs={{0,4},{4,8},{8,12},{12,0},{1,5},{5,9},{9,13},{13,1},{2,6},{6,10},{... | collective-permute-start | bytes 196616 | tf_op jit(solution)/shard_map/ppermute | solution.py:215
  2.3 25.7 %collective-permute-start.11 = (bf16[16,2048]{1,0:T(8,128)(2,1)}, bf16[16,2048]{1,0:T(8,128)(2,1)S(1)}, u32[]{:S(2)}, u32[]{:S(2)}) collective-permute-start(bf16[16,2048]{1,0:T(8,128)(2,1)} %refs_0_.1), channel_id=1, source_target_pairs={{0,8},{4,12},{8,0},{12,4},{1,9},{5,13},{9,1},{13,5},{2,10},{6,14},... | collective-permute-start | bytes 196616 | tf_op jit(solution)/shard_map/ppermute | solution.py:215
  3.5 25.1 %collective-permute-start.12 = (bf16[16,2048]{1,0:T(8,128)(2,1)}, bf16[16,2048]{1,0:T(8,128)(2,1)S(1)}, u32[]{:S(2)}, u32[]{:S(2)}) collective-permute-start(bf16[16,2048]{1,0:T(8,128)(2,1)} %refs_0_.1), channel_id=1, source_target_pairs={{0,12},{4,0},{8,4},{12,8},{1,13},{5,1},{9,5},{13,9},{2,14},{6,2},{... | collective-permute-start | bytes 196616 | tf_op jit(solution)/shard_map/ppermute | solution.py:215
  6.7 31.5 %collective-permute-start.5 = (bf16[2,352,128]{2,1,0:T(8,128)(2,1)S(1)}, bf16[2,352,128]{2,1,0:T(8,128)(2,1)S(1)}, u32[]{:S(2)}, u32[]{:S(2)}) collective-permute-start(bf16[2,352,128]{2,1,0:T(8,128)(2,1)S(1)} %pad_maximum_fusion.3), channel_id=1, source_target_pairs={{0,12},{1,13},{2,14},{3,15},{16,28},{17,29},{18,30},{19,31}} | collective-permute-start | bytes 540680 | tf_op jit(solution)/shard_map/ppermute | solution.py:199
  7.4 32.1 %collective-permute-start.6 = (bf16[2,352,128]{2,1,0:T(8,128)(2,1)S(1)}, bf16[2,352,128]{2,1,0:T(8,128)(2,1)S(1)}, u32[]{:S(2)}, u32[]{:S(2)}) collective-permute-start(bf16[2,352,128]{2,1,0:T(8,128)(2,1)S(1)} %pad_maximum_fusion.4), channel_id=1, source_target_pairs={{0,8},{1,9},{2,10},{3,11},{16,24},{17,25},{18,26},{19,27}} | collective-permute-start | bytes 540680 | tf_op jit(solution)/shard_map/ppermute | solution.py:199
  26.6 2.7 %copy-start.9 = (bf16[16,2048]{1,0:T(8,128)(2,1)}, bf16[16,2048]{1,0:T(8,128)(2,1)S(1)}, u32[]{:S(2)}) copy-start(bf16[16,2048]{1,0:T(8,128)(2,1)S(1)} %collective-permute-done.10.refs_1_) | copy-start | bytes 196612
  26.6 17.9 %collective-permute-start.7 = (bf16[2,352,128]{2,1,0:T(8,128)(2,1)S(1)}, bf16[2,352,128]{2,1,0:T(8,128)(2,1)S(1)}, u32[]{:S(2)}, u32[]{:S(2)}) collective-permute-start(bf16[2,352,128]{2,1,0:T(8,128)(2,1)S(1)} %pad_maximum_fusion.5), channel_id=1, source_target_pairs={{0,4},{1,5},{2,6},{3,7},{16,20},{17,21},{18,22},{19,23}} | collective-permute-start | bytes 540680 | tf_op jit(solution)/shard_map/ppermute | solution.py:199
  27.9 1.4 %copy-start.10 = (bf16[16,2048]{1,0:T(8,128)(2,1)}, bf16[16,2048]{1,0:T(8,128)(2,1)S(1)}, u32[]{:S(2)}) copy-start(bf16[16,2048]{1,0:T(8,128)(2,1)S(1)} %collective-permute-done.11.refs_2_) | copy-start | bytes 196612
  27.9 16.7 %collective-permute-start = (bf16[2,352,128]{2,1,0:T(8,128)(2,1)S(1)}, bf16[2,352,128]{2,1,0:T(8,128)(2,1)S(1)}, u32[]{:S(2)}, u32[]{:S(2)}) collective-permute-start(bf16[2,352,128]{2,1,0:T(8,128)(2,1)S(1)} %pad_maximum_fusion), channel_id=1, source_target_pairs={{0,12},{1,13},{2,14},{3,15},{16,28},{17,29},{18,30},{19,31}} | collective-permute-start | bytes 540680 | tf_op jit(solution)/shard_map/ppermute | solution.py:199
  28.6 0.7 copy-start.11
  28.6 17.6 %collective-permute-start.1 = (bf16[2,352,128]{2,1,0:T(8,128)(2,1)S(1)}, bf16[2,352,128]{2,1,0:T(8,128)(2,1)S(1)}, u32[]{:S(2)}, u32[]{:S(2)}) collective-permute-start(bf16[2,352,128]{2,1,0:T(8,128)(2,1)S(1)} %pad_maximum_fusion.1), channel_id=1, source_target_pairs={{0,8},{1,9},{2,10},{3,11},{16,24},{17,25},{18,26},{19,27}} | collective-permute-start | bytes 540680 | tf_op jit(solution)/shard_map/ppermute | solution.py:199
  38.3 11.8 %collective-permute-start.2 = (bf16[2,352,128]{2,1,0:T(8,128)(2,1)S(1)}, bf16[2,352,128]{2,1,0:T(8,128)(2,1)S(1)}, u32[]{:S(2)}, u32[]{:S(2)}) collective-permute-start(bf16[2,352,128]{2,1,0:T(8,128)(2,1)S(1)} %pad_maximum_fusion.2), channel_id=1, source_target_pairs={{0,4},{1,5},{2,6},{3,7},{16,20},{17,21},{18,22},{19,23}} | collective-permute-start | bytes 540680 | tf_op jit(solution)/shard_map/ppermute | solution.py:199
  39.6 13.5 %collective-permute-start.13 = (f32[1,264,128]{2,1,0:T(8,128)S(1)}, f32[1,264,128]{2,1,0:T(8,128)S(1)}, u32[]{:S(2)}, u32[]{:S(2)}) collective-permute-start(f32[1,264,128]{2,1,0:T(8,128)S(1)} %get-tuple-element.20), channel_id=1, source_target_pairs={{0,12},{4,0},{8,4},{12,8},{1,13},{5,1},{9,5},{13,9},{2,14},{6,2},{... | collective-permute-start | bytes 405512 | tf_op jit(solution)/shard_map/ppermute | solution.py:274
  44.6 11.4 %collective-permute-start.14 = (f32[1,264,128]{2,1,0:T(8,128)S(1)}, f32[1,264,128]{2,1,0:T(8,128)S(1)}, u32[]{:S(2)}, u32[]{:S(2)}) collective-permute-start(f32[1,264,128]{2,1,0:T(8,128)S(1)} %get-tuple-element.19), channel_id=1, source_target_pairs={{0,8},{4,12},{8,0},{12,4},{1,9},{5,13},{9,1},{13,5},{2,10},{6,14},... | collective-permute-start | bytes 405512 | tf_op jit(solution)/shard_map/ppermute | solution.py:274
  44.6 22.4 %copy-start = (bf16[2,352,128]{2,1,0:T(8,128)(2,1)}, bf16[2,352,128]{2,1,0:T(8,128)(2,1)S(1)}, u32[]{:S(2)}) copy-start(bf16[2,352,128]{2,1,0:T(8,128)(2,1)S(1)} %select_select_fusion.refs_0_) | copy-start | bytes 540676
  44.6 15.4 %collective-permute-start.15 = (f32[1,264,128]{2,1,0:T(8,128)S(1)}, f32[1,264,128]{2,1,0:T(8,128)S(1)}, u32[]{:S(2)}, u32[]{:S(2)}) collective-permute-start(f32[1,264,128]{2,1,0:T(8,128)S(1)} %get-tuple-element.18), channel_id=1, source_target_pairs={{0,4},{4,8},{8,12},{12,0},{1,5},{5,9},{9,13},{13,1},{2,6},{6,10},{... | collective-permute-start | bytes 405512 | tf_op jit(solution)/shard_map/ppermute | solution.py:274
  46.2 16.4 %collective-permute-start.8 = (bf16[2,352,128]{2,1,0:T(8,128)(2,1)S(1)}, bf16[2,352,128]{2,1,0:T(8,128)(2,1)S(1)}, u32[]{:S(2)}, u32[]{:S(2)}) collective-permute-start(bf16[2,352,128]{2,1,0:T(8,128)(2,1)S(1)} %select_select_fusion.refs_0_), channel_id=1, source_target_pairs={{4,8},{8,12},{12,4},{5,9},{9,13},{13,5},{6,10},{10,14},{14,6},{7,1... | collective-permute-start | bytes 540680 | tf_op jit(solution)/shard_map/ppermute | solution.py:205
  50.1 16.9 %collective-permute-start.9 = (bf16[2,352,128]{2,1,0:T(8,128)(2,1)S(1)}, bf16[2,352,128]{2,1,0:T(8,128)(2,1)S(1)}, u32[]{:S(2)}, u32[]{:S(2)}) collective-permute-start(bf16[2,352,128]{2,1,0:T(8,128)(2,1)S(1)} %select_select_fusion.refs_0_), channel_id=1, source_target_pairs={{4,12},{8,4},{12,8},{5,13},{9,5},{13,9},{6,14},{10,6},{14,10},{7,1... | collective-permute-start | bytes 540680 | tf_op jit(solution)/shard_map/ppermute | solution.py:205
  53.0 33.7 %copy-start.1 = (bf16[2,352,128]{2,1,0:T(8,128)(2,1)}, bf16[2,352,128]{2,1,0:T(8,128)(2,1)S(1)}, u32[]{:S(2)}) copy-start(bf16[2,352,128]{2,1,0:T(8,128)(2,1)S(1)} %select_select_fusion.1.refs_0_) | copy-start | bytes 540676
  53.0 7.0 %copy-start.6 = (f32[1,264,128]{2,1,0:T(8,128)}, f32[1,264,128]{2,1,0:T(8,128)S(1)}, u32[]{:S(2)}) copy-start(f32[1,264,128]{2,1,0:T(8,128)S(1)} %collective-permute-done.13.refs_1_) | copy-start | bytes 405508
  53.0 33.6 %collective-permute-start.3 = (bf16[2,352,128]{2,1,0:T(8,128)(2,1)S(1)}, bf16[2,352,128]{2,1,0:T(8,128)(2,1)S(1)}, u32[]{:S(2)}, u32[]{:S(2)}) collective-permute-start(bf16[2,352,128]{2,1,0:T(8,128)(2,1)S(1)} %select_select_fusion.1.refs_0_), channel_id=1, source_target_pairs={{4,8},{8,12},{12,4},{5,9},{9,13},{13,5},{6,10},{10,14},{14,6},{7,1... | collective-permute-start | bytes 540680 | tf_op jit(solution)/shard_map/ppermute | solution.py:205
  56.0 4.0 %copy-start.7 = (f32[1,264,128]{2,1,0:T(8,128)}, f32[1,264,128]{2,1,0:T(8,128)S(1)}, u32[]{:S(2)}) copy-start(f32[1,264,128]{2,1,0:T(8,128)S(1)} %collective-permute-done.14.refs_2_) | copy-start | bytes 405508
  56.0 30.7 %collective-permute-start.4 = (bf16[2,352,128]{2,1,0:T(8,128)(2,1)S(1)}, bf16[2,352,128]{2,1,0:T(8,128)(2,1)S(1)}, u32[]{:S(2)}, u32[]{:S(2)}) collective-permute-start(bf16[2,352,128]{2,1,0:T(8,128)(2,1)S(1)} %select_select_fusion.1.refs_0_), channel_id=1, source_target_pairs={{4,12},{8,4},{12,8},{5,13},{9,5},{13,9},{6,14},{10,6},{14,10},{7,1... | collective-permute-start | bytes 540680 | tf_op jit(solution)/shard_map/ppermute | solution.py:205
  60.0 0.7 copy-start.8
  62.7 4.3 %copy-start.2 = (bf16[2,352,128]{2,1,0:T(8,128)(2,1)}, bf16[2,352,128]{2,1,0:T(8,128)(2,1)S(1)}, u32[]{:S(2)}) copy-start(bf16[2,352,128]{2,1,0:T(8,128)(2,1)S(1)} %collective-permute-done.8.refs_1_) | copy-start | bytes 540676
  67.0 0.7 copy-start.3
  86.7 0.7 copy-start.4
  87.4 0.7 copy-start.5
